TPU v7x, 512 devices: a whole 4x4x16 slice. The times are simulated.
512 devices in a mesh: outer: 8 (over x, y_lo), inner: 64 (over z, y_hi, core).
Axes of the slice: x: 4, y: 4 (y_hi: 2, y_lo: 2; y = y_hi * 2 + y_lo), z: 16, core: 2. Of those that a mesh axis runs over, the one named last changes fastest.
Arguments:
- queries: bfloat16 [16384, 2048], P('inner'), may hold values from -128 to 128
- mem_keys: bfloat16 [8192, 2048], P(('outer', 'inner')), may hold values from -4.5 to 4.5
- mem_values: bfloat16 [8192, 2048], P(('outer', 'inner')), may hold values from -6 to 6
Outputs:
- attended: bfloat16 [16384, 2048], P('inner')
- log_total: float32 [16384, 16], P('inner')
All inputs are finite; a program needn't handle non-finite values.
Results may differ from a plain program's by a relative error of at most 0.014.
Values may be sent and summed in bfloat16 or wider, within the bound.
No kernel may reach another device: no remote copies, remote signals or barrier semaphores. Data moves between devices by JAX's collectives and lax.ppermute only.
A program may use at most 64 MiB of HBM per device.

v0:
```python
import math
import jax
import jax.numpy as jnp
from jax import lax
from jax.sharding import PartitionSpec as P

HEADS = 16
HEAD_DIM = 128


def on_device(queries, mem_keys, mem_values):
    row_count = queries.shape[0]
    columns = queries.shape[1]
    scale = 1.0 / math.sqrt(HEAD_DIM)
    query_heads = queries.reshape(row_count, HEADS, HEAD_DIM)
    initial = (
        jnp.full((row_count, HEADS), -jnp.inf, jnp.float32),
        jnp.zeros((row_count, HEADS), jnp.float32),
        jnp.zeros((row_count, HEADS, HEAD_DIM), jnp.float32),
    )
    key_piece = lax.all_gather(mem_keys, "inner", axis=0, tiled=True)
    value_piece = lax.all_gather(mem_values, "inner", axis=0, tiled=True)
    entries = key_piece.shape[0]
    block = math.gcd(entries, 256)
    key_blocks = key_piece.reshape(entries // block, block, HEADS, HEAD_DIM)
    value_blocks = value_piece.reshape(entries // block, block, HEADS, HEAD_DIM)

    def one_block(running, blocks):
        running_top, running_total, running_out = running
        key_block, value_block = blocks
        scores = (
            jnp.einsum("thd,khd->thk", query_heads, key_block, preferred_element_type=jnp.float32)
            * scale
        )
        new_top = jnp.maximum(running_top, jnp.max(scores, axis=-1))
        fading = jnp.exp(running_top - new_top)
        raw = jnp.exp(scores - new_top[..., None])
        new_total = running_total * fading + jnp.sum(raw, axis=-1)
        product = jnp.einsum(
            "thk,khd->thd",
            raw.astype(jnp.bfloat16),
            value_block,
            preferred_element_type=jnp.float32,
        )
        new_out = running_out * fading[..., None] + product
        return ((new_top, new_total, new_out), None)

    result, unused = lax.scan(one_block, initial, (key_blocks, value_blocks))
    group_peak, group_total, group_out = result
    peak = lax.pmax(group_peak, "outer")
    factor = jnp.exp(group_peak - peak)
    weighted = (group_out * factor[..., None]).reshape(row_count, columns)
    total = lax.psum(group_total * factor, "outer")
    log_total = peak + jnp.log(total)
    summed = lax.psum(weighted.astype(jnp.bfloat16), "outer").astype(jnp.float32)
    attended = (
        (summed.reshape(row_count, HEADS, HEAD_DIM) / total[..., None])
        .astype(jnp.bfloat16)
        .reshape(row_count, columns)
    )
    return (attended, log_total)


def solution(mesh):
    in_specs = (P("inner", None), P(("outer", "inner"), None), P(("outer", "inner"), None))
    out_specs = (P("inner", None), P("inner", None))
    return jax.shard_map(
        on_device, mesh=mesh, in_specs=in_specs, out_specs=out_specs, check_vma=False
    )
```

profile of v0, /device:TPU:32, one launch (start us, length us, event | category | flops | bytes accessed | tf_op | source)
XLA Modules:
  0.0 486.1 jit_solution(9600157572781027679)
XLA Ops:
  8.7 1.5 copy.9
  10.2 1.3 copy.11
  11.5 154.5 %all-gather.3.cloned.1.call-done = bf16[1024,2048]{1,0:T(8,128)(2,1)} async-done(((bf16[16,2048]{1,0:T(8,128)(2,1)}), bf16[1024,2048]{1,0:T(8,128)(2,1)}) %all-gather.3.cloned.1.call-update) | async-done | bytes 4194320 | tf_op jit(solution)/shard_map/all_gather | solution.py:21
  166.0 5.5 %copy.19 = bf16[128,8,16,128]{3,2,1,0:T(8,128)(2,1)} copy(bf16[128,8,16,128]{3,1,2,0:T(8,128)(2,1)} %bitcast.54) | data formatting | bytes 8388608
  171.6 142.9 %all-gather.5.cloned.1.call-done = bf16[1024,2048]{1,0:T(8,128)(2,1)} async-done(((bf16[16,2048]{1,0:T(8,128)(2,1)}), bf16[1024,2048]{1,0:T(8,128)(2,1)}) %all-gather.5.cloned.1.call-update) | async-done | bytes 4194320 | tf_op jit(solution)/shard_map/all_gather | solution.py:22
  314.4 5.6 %copy.20 = bf16[128,8,16,128]{3,2,1,0:T(8,128)(2,1)} copy(bf16[128,8,16,128]{3,1,2,0:T(8,128)(2,1)} %bitcast.55) | data formatting | bytes 8388608
  320.0 33.2 %while.15 = (s32[]{:T(128)}, f32[256,16]{0,1:T(8,128)S(1)}, f32[256,16]{0,1:T(8,128)S(1)}, f32[256,16,128]{0,2,1:T(8,128)}, bf16[4,256,16,128]{3,2,1,0:T(8,128)(...) while((s32[]{:T(128)}, f32[256,16]{0,1:T(8,128)S(1)}, ...), condition=%wide.region_3.4_spmd.clone, body=%wide.region_0.3_spmd.clone.sunk | while | flops 546852864 | bytes 43253932 | solution.py:48
  320.0 1.9 constant_dynamic-slice_fusion.3
  321.9 0.8 copy.30
  322.7 2.1 bitcast_reduce_fusion.2
  325.6 1.4 bitcast_add_fusion.2
  327.0 1.3 copy-done.1
  328.3 1.9 constant_dynamic-slice_fusion.3
  330.2 0.8 copy.30
  331.0 2.1 bitcast_reduce_fusion.2
  333.9 1.4 bitcast_add_fusion.2
  335.3 1.3 copy-done.1
  336.6 1.9 constant_dynamic-slice_fusion.3
  338.5 0.8 copy.30
  339.3 2.1 bitcast_reduce_fusion.2
  342.2 1.4 bitcast_add_fusion.2
  343.6 1.3 copy-done.1
  344.9 1.9 constant_dynamic-slice_fusion.3
  347.6 2.1 bitcast_reduce_fusion.2
  350.5 1.4 bitcast_add_fusion.2
  351.9 1.3 copy-done.1
  353.2 33.2 %pmax.7 = f32[256,16]{0,1:T(8,128)S(1)} all-reduce(f32[256,16]{0,1:T(8,128)S(1)} %get-tuple-element.42), channel_id=1, replica_groups=mesh['outer'=8,'inner'=64] {'outer'}, use_global_device_ids=true, to_apply=%region_4.5 | all-reduce | flops 4096 | bytes 32768 | tf_op jit(solution)/shard_map/pmax | solution.py:50
  386.4 1.8 multiply_convert_fusion
  388.2 1.4 copy.16
  389.6 31.2 %psum.15 = f32[256,16]{0,1:T(8,128)S(1)} all-reduce(f32[256,16]{0,1:T(8,128)S(1)} %get-tuple-element.91), channel_id=1, replica_groups=mesh['outer'=8,'inner'=64] {'outer'}, use_global_device_ids=true, to_apply=%region_6.7 | all-reduce | flops 4096 | bytes 32768 | tf_op jit(solution)/shard_map/psum | solution.py:53
  421.6 54.3 %all-reduce.2.cloned.1.call-done = bf16[256,2048]{1,0:T(8,128)(2,1)} async-done(((bf16[256,2048]{1,0:T(8,128)(2,1)}), bf16[256,2048]{1,0:T(8,128)(2,1)}) %all-reduce.2.cloned.1.call-update) | async-done | bytes 1048592 | tf_op jit(solution)/shard_map/psum | solution.py:55
  476.5 3.1 fusion.13
  (42 shorter events, 6.6 us)
Async XLA Ops:
  7.2 158.9 %all-gather.3.cloned.1.call-start = ((), (), s32[]{:S(2)}) async-start(), calls=%async_computation | async-start | bytes 4259840 | tf_op jit(solution)/shard_map/all_gather | solution.py:21
  7.9 306.5 %all-gather.5.cloned.1.call-start = ((), (), s32[]{:S(2)}) async-start(), calls=%async_computation.1 | async-start | bytes 4259840 | tf_op jit(solution)/shard_map/all_gather | solution.py:22
  8.6 467.2 %all-reduce.2.cloned.1.call-start = ((), (), s32[]{:S(2)}) async-start(), calls=%async_computation.2 | async-start | bytes 2097152 | tf_op jit(solution)/shard_map/psum | solution.py:55
  322.7 2.9 copy-start
  326.9 1.3 copy-start.1
  331.0 2.9 copy-start
  335.2 1.3 copy-start.1
  339.3 2.9 copy-start
  343.5 1.3 copy-start.1
  347.6 2.9 copy-start
  351.8 1.3 copy-start.1
Sparse Core Ops, SparseCore 0:
  11.3 154.7 all-gather.2
  169.3 145.0 all-gather.4
  389.7 86.0 all-reduce.1
where the time goes:
time: 487 us; the launch traced here: 486 us
  waiting for transfers between devices  353 us (72%)
  blocking collectives  64.4 us (13%)
  local copies, waits for them, and re-layouts  32.1 us (7%)
  matrix products  13.9 us (3%)
  between operations  13.8 us (3%)
  other arithmetic  8.47 us (2%)
    all_gather x1, waiting for transfers between devices, on_device(): key_piece = lax.all_gather(mem_keys, 'inner', axis=0, tiled=True)  154 us
    all_gather x1, waiting for transfers between devices, on_device(): value_piece = lax.all_gather(mem_values, 'inner', axis=0, tiled=True)  143 us
    psum x1, waiting for transfers between devices, on_device(): lax.psum(weighted.astype(jnp.bfloat16), 'outer').astype(jnp.float32)  54.3 us
    pmax x1, blocking collectives, on_device(): peak = lax.pmax(group_peak, 'outer')  33.2 us
    psum x1, blocking collectives, on_device(): total = lax.psum(group_total * factor, 'outer')  31.2 us
    unnamed x4, local copies, waits for them, and re-layouts  13.9 us
    dynamic_slice x8, local copies, waits for them, and re-layouts, on_device(): result, unused = lax.scan(one_block, initial, (key_blocks, value_blocks))  10.8 us
  transfers between devices with their start and end apart: 3, of which 3 were waited for; matrix products, arithmetic and copies ran while one was open for 2% of the time, Pallas kernels for 0%

commit v1 on v0

--- a/solution.py
+++ b/solution.py
@@ -19,7 +19,9 @@
         jnp.zeros((row_count, HEADS, HEAD_DIM), jnp.float32),
     )
     key_piece = lax.all_gather(mem_keys, "inner", axis=0, tiled=True)
-    value_piece = lax.all_gather(mem_values, "inner", axis=0, tiled=True)
+    value_piece = jnp.concatenate(
+        lax.all_to_all(jnp.stack([mem_values] * lax.axis_size("inner")), "inner", 0, 0), axis=0
+    )
     entries = key_piece.shape[0]
     block = math.gcd(entries, 256)
     key_blocks = key_piece.reshape(entries // block, block, HEADS, HEAD_DIM)

time: 487 us -> 413 us (0.85)
  waiting for transfers between devices: 353 us -> 258 us
  starting transfers between devices: 0.11 us -> 18.8 us
    all_gather x1 -> x0, waiting for transfers between devices: 143 us -> none  [on_device(): value_piece = lax.all_gather(mem_values, 'inner', axis=0, tiled=True)]
    all_gather x1, waiting for transfers between devices: 154 us -> 197 us  [on_device(): key_piece = lax.all_gather(mem_keys, 'inner', axis=0, tiled=True)]
    all_to_all x0 -> x1, starting transfers between devices: none -> 18.7 us  [on_device(): lax.all_to_all(jnp.stack([mem_values] * lax.axis_size('inner')), 'inner',...]
    psum x1, waiting for transfers between devices: 54.3 us -> 59.9 us  [on_device(): lax.psum(weighted.astype(jnp.bfloat16), 'outer').astype(jnp.float32)]
    unnamed x4 -> x6, local copies, waits for them, and re-layouts: 13.9 us -> 12.9 us
where the time goes in v1:
time: 413 us; the launch traced here: 412 us
  waiting for transfers between devices  258 us (62%)
  blocking collectives  63.9 us (15%)
  local copies, waits for them, and re-layouts  34.5 us (8%)
  starting transfers between devices  18.8 us (5%)
  between operations  14.1 us (3%)
  matrix products  13.9 us (3%)
  other arithmetic  8.47 us (2%)
    all_gather x1, waiting for transfers between devices, on_device(): key_piece = lax.all_gather(mem_keys, 'inner', axis=0, tiled=True)  197 us
    psum x1, waiting for transfers between devices, on_device(): lax.psum(weighted.astype(jnp.bfloat16), 'outer').astype(jnp.float32)  59.9 us
    pmax x1, blocking collectives, on_device(): peak = lax.pmax(group_peak, 'outer')  33.2 us
    psum x1, blocking collectives, on_device(): total = lax.psum(group_total * factor, 'outer')  30.7 us
    all_to_all x1, starting transfers between devices, on_device(): lax.all_to_all(jnp.stack([mem_values] * lax.axis_size('inner')), 'inner',...  18.7 us
    unnamed x6, local copies, waits for them, and re-layouts  12.9 us
    dynamic_slice x8, local copies, waits for them, and re-layouts, on_device(): result, unused = lax.scan(one_block, initial, (key_blocks, value_blocks))  10.8 us
    dot_general x4, matrix products, one_block(): jnp.einsum('thd,khd->thk', query_heads, key_block, preferred_element_type...  8.38 us
  transfers between devices with their start and end apart: 3, of which 3 were waited for; matrix products, arithmetic and copies ran while one was open for 2% of the time, Pallas kernels for 0%

profile of v1, /device:TPU:32, one launch (start us, length us, event | category | flops | bytes accessed | tf_op | source)
XLA Modules:
  0.0 412.0 jit_solution(16932424578292645740)
XLA Ops:
  7.2 3.3 stack.2
  10.5 18.7 %all-to-all-start = ((bf16[64,16,2048]{2,1,0:T(8,128)(2,1)}), bf16[64,16,2048]{2,1,0:T(8,128)(2,1)}, u32[]{:S(2)}, u32[]{:S(2)}) async-start(bf16[64,16,2048]{2,1,0:T(8,128)(2,1)} %stack.2), calls=%async_computation | async-start | bytes 8388608 | tf_op jit(solution)/shard_map/all_to_all | solution.py:23
  30.6 1.3 copy.11
  31.9 196.8 %all-gather.2.cloned.1.call-done = bf16[1024,2048]{1,0:T(8,128)(2,1)} async-done(((bf16[16,2048]{1,0:T(8,128)(2,1)}), bf16[1024,2048]{1,0:T(8,128)(2,1)}) %all-gather.2.cloned.1.call-update) | async-done | bytes 4194320 | tf_op jit(solution)/shard_map/all_gather | solution.py:21
  228.7 5.5 %copy.19 = bf16[128,8,16,128]{3,2,1,0:T(8,128)(2,1)} copy(bf16[128,8,16,128]{3,1,2,0:T(8,128)(2,1)} %bitcast.55) | data formatting | bytes 8388608
  234.9 5.6 %copy.20 = bf16[128,8,16,128]{3,2,1,0:T(8,128)(2,1)} copy(bf16[128,8,16,128]{3,1,2,0:T(8,128)(2,1)} %bitcast.10) | data formatting | bytes 8388608
  240.5 33.2 %while.15 = (s32[]{:T(128)}, f32[256,16]{0,1:T(8,128)S(1)}, f32[256,16]{0,1:T(8,128)S(1)}, f32[256,16,128]{0,2,1:T(8,128)}, bf16[4,256,16,128]{3,2,1,0:T(8,128)(...) while((s32[]{:T(128)}, f32[256,16]{0,1:T(8,128)S(1)}, ...), condition=%wide.region_3.4_spmd.clone, body=%wide.region_0.3_spmd.clone.sunk | while | flops 546852864 | bytes 43253932 | solution.py:50
  240.5 1.9 constant_dynamic-slice_fusion.3
  242.4 0.8 copy.30
  243.2 2.1 bitcast_reduce_fusion.2
  246.1 1.4 bitcast_add_fusion.2
  247.4 1.3 copy-done.1
  248.8 1.9 constant_dynamic-slice_fusion.3
  250.7 0.8 copy.30
  251.5 2.1 bitcast_reduce_fusion.2
  254.3 1.4 bitcast_add_fusion.2
  255.7 1.3 copy-done.1
  257.1 1.9 constant_dynamic-slice_fusion.3
  259.0 0.8 copy.30
  259.8 2.1 bitcast_reduce_fusion.2
  262.6 1.4 bitcast_add_fusion.2
  264.0 1.3 copy-done.1
  265.4 1.9 constant_dynamic-slice_fusion.3
  268.1 2.1 bitcast_reduce_fusion.2
  270.9 1.4 bitcast_add_fusion.2
  272.3 1.3 copy-done.1
  273.7 33.2 %pmax.7 = f32[256,16]{0,1:T(8,128)S(1)} all-reduce(f32[256,16]{0,1:T(8,128)S(1)} %get-tuple-element.42), channel_id=1, replica_groups=mesh['outer'=8,'inner'=64] {'outer'}, use_global_device_ids=true, to_apply=%region_4.5 | all-reduce | flops 4096 | bytes 32768 | tf_op jit(solution)/shard_map/pmax | solution.py:52
  306.8 1.8 multiply_convert_fusion
  308.6 1.4 copy.16
  310.1 30.7 %psum.15 = f32[256,16]{0,1:T(8,128)S(1)} all-reduce(f32[256,16]{0,1:T(8,128)S(1)} %get-tuple-element.91), channel_id=1, replica_groups=mesh['outer'=8,'inner'=64] {'outer'}, use_global_device_ids=true, to_apply=%region_6.7 | all-reduce | flops 4096 | bytes 32768 | tf_op jit(solution)/shard_map/psum | solution.py:55
  341.5 59.9 %all-reduce.2.cloned.1.call-done = bf16[256,2048]{1,0:T(8,128)(2,1)} async-done(((bf16[256,2048]{1,0:T(8,128)(2,1)}), bf16[256,2048]{1,0:T(8,128)(2,1)}) %all-reduce.2.cloned.1.call-update) | async-done | bytes 1048592 | tf_op jit(solution)/shard_map/psum | solution.py:57
  402.1 3.1 fusion.13
  (44 shorter events, 7.1 us)
Async XLA Ops:
  10.5 19.5 %copy-start.2 = (bf16[256,2048]{1,0:T(8,128)(2,1)S(1)}, bf16[256,2048]{1,0:T(8,128)(2,1)}, u32[]{:S(2)}) copy-start(bf16[256,2048]{1,0:T(8,128)(2,1)} %param.5) | copy-start | bytes 3145732
  10.5 224.4 %all-to-all-start = ((bf16[64,16,2048]{2,1,0:T(8,128)(2,1)}), bf16[64,16,2048]{2,1,0:T(8,128)(2,1)}, u32[]{:S(2)}, u32[]{:S(2)}) async-start(bf16[64,16,2048]{2,1,0:T(8,128)(2,1)} %stack.2), calls=%async_computation | async-start | bytes 8388608 | tf_op jit(solution)/shard_map/all_to_all | solution.py:23
  29.2 199.4 %all-gather.2.cloned.1.call-start = ((), (), s32[]{:S(2)}) async-start(), calls=%async_computation.1 | async-start | bytes 4259840 | tf_op jit(solution)/shard_map/all_gather | solution.py:21
  29.9 371.5 %all-reduce.2.cloned.1.call-start = ((), (), s32[]{:S(2)}) async-start(), calls=%async_computation.2 | async-start | bytes 2097152 | tf_op jit(solution)/shard_map/psum | solution.py:57
  243.2 2.9 copy-start
  247.4 1.3 copy-start.1
  251.5 2.9 copy-start
  255.7 1.3 copy-start.1
  259.8 2.9 copy-start
  264.0 1.3 copy-start.1
  268.1 2.9 copy-start
  272.3 1.3 copy-start.1
Sparse Core Ops, SparseCore 0:
  33.3 195.2 all-gather.1
  310.2 91.1 all-reduce.1
